TPU v7x, 512 devices: a whole 4x8x8 slice. The times are simulated.
512 devices in a mesh: section: 16 (over x, y_lo, core), tensor: 32 (over y_hi, z).
Axes of the slice: x: 4, y: 8 (y_hi: 4, y_lo: 2; y = y_hi * 2 + y_lo), z: 8, core: 2. Of those that a mesh axis runs over, the one named last changes fastest.
Arguments:
- hidden: bfloat16 [16, 256, 8192], P('section', 'tensor'), may hold values from -60 to 60
- norm_gain: float32 [8192], replicated, may hold values from 0.1 to 1.9
- lengths: int32 [16], P('section'), may hold values from 64 to 256
- query_param: float32 [8192, 4096], P(('section', 'tensor')), may hold values from -1.3258252 to 1.3258252
- query_grad: float32 [8192, 4096], P(('section', 'tensor')), may hold values from -0.006 to 0.006
- query_moment: float32 [8192, 4096], P(('section', 'tensor')), may hold values from -0.006 to 0.006
- query_second: float32 [8192, 4096], P(('section', 'tensor')), may hold values from 1e-07 to 1e-05
- keyval_param: float32 [8192, 1024], P(('section', 'tensor')), may hold values from -0.06629126 to 0.06629126
- keyval_gradient: float32 [8192, 1024], P(('section', 'tensor')), may hold values from -0.006 to 0.006
- keyval_first_moment: float32 [8192, 1024], P(('section', 'tensor')), may hold values from -0.006 to 0.006
- keyval_second_moment: float32 [8192, 1024], P(('section', 'tensor')), may hold values from 1e-07 to 1e-05
- output_param: float32 [8192, 4096], P(('section', 'tensor')), may hold values from -0.25 to 0.25
- output_grad: float32 [8192, 4096], P(('section', 'tensor')), may hold values from -0.006 to 0.006
- output_moment: float32 [8192, 4096], P(('section', 'tensor')), may hold values from -0.006 to 0.006
- output_second: float32 [8192, 4096], P(('section', 'tensor')), may hold values from 1e-07 to 1e-05
Outputs:
- mixed: bfloat16 [16, 256, 8192], P('section', 'tensor')
All inputs are finite; a program needn't handle non-finite values.
Results may differ from a plain program's by a relative error of at most 0.017.
Values may be sent and summed in bfloat16 or wider, within the bound.
No kernel may reach another device: no remote copies, remote signals or barrier semaphores. Data moves between devices by JAX's collectives and lax.ppermute only.
A program may use at most 64 MiB of HBM per device.

v0:
```python
import math

import jax
import jax.numpy as jnp
from jax import lax
from jax.sharding import PartitionSpec as P

QUERY_HEADS_LOCAL = 32
KEYVAL_HEADS = 4
HEAD_DIMENSION = 128


learn_rate = 0.015
beta_one = 0.5
beta_two = 0.9
adam_step = 1000.0
adam_eps = 1e-08
decay_rate = 0.1
norm_eps = 1e-06
rope_base = 1000000.0
masked_score = -1e30


def adam_update(current, gradient, moment, second):
    moment_new = beta_one * moment + (1.0 - beta_one) * gradient
    second_new = beta_two * second + (1.0 - beta_two) * gradient * gradient
    corrected = moment_new / (1.0 - beta_one**adam_step)
    denominator = jnp.sqrt(second_new / (1.0 - beta_two**adam_step)) + adam_eps
    return (current - learn_rate * (corrected / denominator + decay_rate * current)).astype(
        jnp.bfloat16
    )


def normalize(hidden, norm_gain):
    values = hidden.astype(jnp.float32)
    factor = lax.rsqrt(jnp.mean(values * values, axis=-1, keepdims=True) + norm_eps)
    return (values * factor * norm_gain).astype(jnp.bfloat16)


def rotary_embed(values, token_positions):
    half_width = values.shape[-1] // 2
    frequency = rope_base ** (-jnp.arange(half_width, dtype=jnp.float32) * 2.0 / values.shape[-1])
    angles = token_positions.astype(jnp.float32)[:, None] * frequency[None, :]
    cosine_table = jnp.concatenate([jnp.cos(angles), jnp.cos(angles)], axis=-1)
    sine_table = jnp.concatenate([jnp.sin(angles), jnp.sin(angles)], axis=-1)
    first_half = values[..., :half_width]
    second_half = values[..., half_width:]
    rotated = jnp.concatenate([-second_half, first_half], axis=-1)
    return values * cosine_table + rotated * sine_table


def on_device(
    hidden,
    norm_gain,
    lengths,
    query_param,
    query_grad,
    query_moment,
    query_second,
    keyval_param,
    keyval_gradient,
    keyval_first_moment,
    keyval_second_moment,
    output_param,
    output_grad,
    output_moment,
    output_second,
):
    tensor_count = lax.axis_size("tensor")
    query_weight = adam_update(query_param, query_grad, query_moment, query_second)
    keyval_matrix = adam_update(
        keyval_param, keyval_gradient, keyval_first_moment, keyval_second_moment
    )
    output_weight = adam_update(output_param, output_grad, output_moment, output_second)
    local_rows = normalize(hidden[0], norm_gain)
    normed = lax.all_gather(local_rows, "tensor", axis=0, tiled=True)
    sequence = normed.shape[0]
    model_width = normed.shape[1]
    weight_row_block = query_weight.shape[0]
    heads_here = QUERY_HEADS_LOCAL // tensor_count
    head_columns = heads_here * HEAD_DIMENSION
    head_copies = tensor_count // KEYVAL_HEADS
    spread_heads = keyval_matrix.reshape(weight_row_block, 2, KEYVAL_HEADS, HEAD_DIMENSION)
    spread_heads = (
        jnp.repeat(spread_heads, head_copies, axis=2)
        .transpose(0, 2, 1, 3)
        .reshape(weight_row_block, tensor_count * 2 * HEAD_DIMENSION)
    )
    keyval_columns = spread_heads.shape[1] // tensor_count
    query_start = jnp.zeros((sequence, head_columns), jnp.float32)
    keyval_start = jnp.zeros((sequence, keyval_columns), jnp.float32)
    query_slice, keyval_slice, output_slice = (
        lax.all_to_all(query_weight, "tensor", split_axis=1, concat_axis=0, tiled=True),
        lax.all_to_all(spread_heads, "tensor", split_axis=1, concat_axis=0, tiled=True),
        lax.all_to_all(output_weight, "tensor", split_axis=1, concat_axis=0, tiled=True),
    )
    initial = (query_start, keyval_start, jnp.zeros((model_width, head_columns), jnp.bfloat16))
    offset = jnp.int32(0)
    query_total = initial[0]
    query_rows = lax.all_gather(query_slice, "section", axis=0, tiled=True)
    keyval_rows = lax.all_gather(keyval_slice, "section", axis=0, tiled=True)
    columns = lax.dynamic_slice_in_dim(normed, offset, query_rows.shape[0], 1)
    query_total = query_total + jnp.dot(columns, query_rows, preferred_element_type=jnp.float32)
    keyval_total = jnp.dot(columns, keyval_rows, preferred_element_type=jnp.float32)
    query_total, keyval_total = (query_total, keyval_total)
    out_buffer = lax.dynamic_update_slice_in_dim(
        initial[2], lax.all_gather(output_slice, "section", axis=0, tiled=True), offset, 0
    )
    key_block = keyval_total[:, :HEAD_DIMENSION]
    value_block = keyval_total[:, HEAD_DIMENSION:]
    token_positions = jnp.arange(sequence)
    query_heads = rotary_embed(
        query_total.reshape(sequence, heads_here, HEAD_DIMENSION).transpose(1, 0, 2),
        token_positions,
    ).astype(jnp.bfloat16)
    key_head_rows = rotary_embed(key_block, token_positions).astype(jnp.bfloat16)
    value_head_rows = value_block.astype(jnp.bfloat16)
    scores = jnp.einsum(
        "hqd,kd->hqk", query_heads, key_head_rows, preferred_element_type=jnp.float32
    ) / math.sqrt(HEAD_DIMENSION)
    allowed = (token_positions[None, :] <= token_positions[:, None]) & (
        token_positions[None, :] < lengths[0]
    )
    scores = jnp.where(allowed[None], scores, masked_score)
    row_max = jnp.max(scores, axis=-1, keepdims=True)
    exponent = jnp.exp(scores - row_max)
    attention = (exponent / jnp.sum(exponent, axis=-1, keepdims=True)).astype(jnp.bfloat16)
    head_out = jnp.einsum(
        "hqk,kd->hqd", attention, value_head_rows, preferred_element_type=jnp.float32
    ).astype(jnp.bfloat16)
    head_out = head_out.transpose(1, 0, 2).reshape(sequence, head_columns)
    mixed = lax.psum_scatter(
        lax.dot_general(
            head_out, out_buffer, (((1,), (1,)), ((), ())), preferred_element_type=jnp.float32
        ).astype(jnp.bfloat16),
        "tensor",
        scatter_dimension=0,
        tiled=True,
    )
    return mixed[None]


def solution(mesh):
    return jax.shard_map(
        on_device,
        mesh=mesh,
        in_specs=(
            P("section", "tensor", None),
            P(),
            P("section"),
            P(("section", "tensor"), None),
            P(("section", "tensor"), None),
            P(("section", "tensor"), None),
            P(("section", "tensor"), None),
            P(("section", "tensor"), None),
            P(("section", "tensor"), None),
            P(("section", "tensor"), None),
            P(("section", "tensor"), None),
            P(("section", "tensor"), None),
            P(("section", "tensor"), None),
            P(("section", "tensor"), None),
            P(("section", "tensor"), None),
        ),
        out_specs=P("section", "tensor", None),
        check_vma=False,
    )
```

profile of v0, /device:TPU:6, one launch (start us, length us, event | category | flops | bytes accessed | tf_op | source)
XLA Modules:
  0.0 503.8 jit_solution(8124403716524646474)
XLA Ops:
  6.5 0.0 copy-start
  6.5 0.0 copy-start.1
  6.5 0.0 copy-start.3
  6.5 0.0 copy-start.2
  6.5 0.0 all-gather.7.cloned.1.call-start
  6.6 1.5 copy_bitcast_fusion.1
  8.0 28.5 %all_to_all.57 = bf16[16,32,128]{2,0,1:T(8,128)(2,1)} all-to-all(bf16[16,32,128]{2,0,1:T(8,128)(2,1)S(1)} %copy_bitcast_fusion.1), channel_id=1, replica_groups=mesh['section'=16,'tensor'=32] {'tensor'}, dimensions={1} | all-to-all | bytes 262144 | tf_op jit(solution)/shard_map/all_to_all | solution.py:93
  36.5 0.0 all-gather.7.cloned.1.call-update
  36.5 0.0 all-gather.5.cloned.1.call-start
  36.6 1.1 fusion.1
  37.7 1.7 fusion.3
  39.3 0.0 all-gather.5.cloned.1.call-update
  39.4 0.0 all-gather.9.cloned.1.call-start
  39.4 1.0 fusion.44
  40.5 0.1 broadcast_in_dim.7
  40.6 0.2 all_to_all.46
  40.8 0.2 copy.24
  41.0 19.7 %all_to_all.58 = bf16[16,32,256]{2,0,1:T(8,128)(2,1)} all-to-all(bf16[16,32,256]{2,0,1:T(8,128)(2,1)S(1)} %copy.24), channel_id=1, replica_groups=mesh['section'=16,'tensor'=32] {'tensor'}, dimensions={1} | all-to-all | bytes 524288 | tf_op jit(solution)/shard_map/all_to_all | solution.py:94
  60.6 0.0 all-gather.9.cloned.1.call-update
  60.7 0.0 all-gather.11.cloned.1.call-start
  60.7 0.0 copy-done
  60.7 0.0 copy-done.1
  60.7 0.0 copy-done.3
  60.7 0.0 copy-done.2
  60.8 0.2 copy_bitcast_fusion
  61.0 17.6 %all_to_all.59 = bf16[16,32,128]{2,0,1:T(8,128)(2,1)} all-to-all(bf16[16,32,128]{2,0,1:T(8,128)(2,1)S(1)} %copy_bitcast_fusion), channel_id=1, replica_groups=mesh['section'=16,'tensor'=32] {'tensor'}, dimensions={1} | all-to-all | bytes 262144 | tf_op jit(solution)/shard_map/all_to_all | solution.py:95
  78.6 0.0 all-gather.11.cloned.1.call-update
  78.6 0.0 reduce-scatter.2.cloned.1.call-start
  79.3 0.3 multiply_sine_fusion
  79.6 0.0 all-gather.7.cloned.1.call-done
  79.7 96.7 %all-gather.5.cloned.1.call-done = bf16[256,8192]{1,0:T(8,128)(2,1)} async-done(((bf16[8,8192]{1,0:T(8,128)(2,1)}), bf16[256,8192]{1,0:T(8,128)(2,1)}) %all-gather.5.cloned.1.call-update) | async-done | bytes 4194320 | tf_op jit(solution)/shard_map/all_gather | solution.py:76
  176.3 4.4 fusion.47
  180.7 34.9 %all-gather.9.cloned.1.call-done = bf16[8192,256]{1,0:T(8,128)(2,1)} async-done(((bf16[512,256]{1,0:T(8,128)(2,1)}), bf16[8192,256]{1,0:T(8,128)(2,1)}) %all-gather.9.cloned.1.call-update) | async-done | bytes 4194320 | tf_op jit(solution)/shard_map/all_gather | solution.py:101
  215.6 5.2 %fusion.48 = f32[256,256]{0,1:T(8,128)S(1)} fusion(bf16[256,8192]{1,0:T(8,128)(2,1)} %all-gather.5.cloned.1.call-done, bf16[8192,256]{1,0:T(8,128)(2,1)} %all-gather.9.cloned.1.call-done), kind=kOutput, calls=%fused_computation.71 | convolution fusion | flops 1073741824 | bytes 8650752 | tf_op jit(solution)/shard_map/dot_general | solution.py:104
  220.8 0.3 fusion.46
  221.1 0.1 fusion.21
  221.1 35.8 %all-gather.11.cloned.1.call-done = bf16[8192,128]{1,0:T(8,128)(2,1)} async-done(((bf16[512,128]{1,0:T(8,128)(2,1)}), bf16[8192,128]{1,0:T(8,128)(2,1)}) %all-gather.11.cloned.1.call-update) | async-done | bytes 2097168 | tf_op jit(solution)/shard_map/all_gather | solution.py:107
  256.9 5.0 convolution_convert_fusion
  261.8 0.0 reduce-scatter.2.cloned.1.call-update
  261.9 235.4 %reduce-scatter.2.cloned.1.call-done = bf16[8,8192]{1,0:T(8,128)(2,1)} async-done(((bf16[256,8192]{1,0:T(8,128)(2,1)}), bf16[8,8192]{1,0:T(8,128)(2,1)}) %reduce-scatter.2.cloned.1.call-update) | async-done | bytes 131088 | tf_op jit(solution)/shard_map/reduce_scatter | solution.py:132
  (8 shorter events, 0.1 us)
Async XLA Ops:
  6.5 54.2 %copy-start = (f32[16,4096]{1,0:T(8,128)S(1)}, f32[16,4096]{1,0:T(8,128)}, u32[]{:S(2)}) copy-start(f32[16,4096]{1,0:T(8,128)} %param.26) | copy-start | bytes 786436
  6.5 54.2 %copy-start.1 = (f32[16,4096]{1,0:T(8,128)S(1)}, f32[16,4096]{1,0:T(8,128)}, u32[]{:S(2)}) copy-start(f32[16,4096]{1,0:T(8,128)} %param.27) | copy-start | bytes 786436
  6.5 54.2 %copy-start.3 = (f32[16,4096]{1,0:T(8,128)S(1)}, f32[16,4096]{1,0:T(8,128)}, u32[]{:S(2)}) copy-start(f32[16,4096]{1,0:T(8,128)} %param.28) | copy-start | bytes 786436
  6.5 54.2 %copy-start.2 = (f32[16,4096]{1,0:T(8,128)S(1)}, f32[16,4096]{1,0:T(8,128)}, u32[]{:S(2)}) copy-start(f32[16,4096]{1,0:T(8,128)} %param.29) | copy-start | bytes 786436
  6.5 73.1 %all-gather.7.cloned.1.call-start = ((), (), s32[]{:S(2)}) async-start(), calls=%async_computation.5 | async-start | bytes 2228224 | tf_op jit(solution)/shard_map/all_gather | solution.py:100
  36.5 139.8 %all-gather.5.cloned.1.call-start = ((), (), s32[]{:S(2)}) async-start(), calls=%async_computation.4 | async-start | bytes 4325376 | tf_op jit(solution)/shard_map/all_gather | solution.py:76
  39.4 176.2 %all-gather.9.cloned.1.call-start = ((), (), s32[]{:S(2)}) async-start(), calls=%async_computation.6 | async-start | bytes 4456448 | tf_op jit(solution)/shard_map/all_gather | solution.py:101
  60.7 196.2 %all-gather.11.cloned.1.call-start = ((), (), s32[]{:S(2)}) async-start(), calls=%async_computation.7 | async-start | bytes 2228224 | tf_op jit(solution)/shard_map/all_gather | solution.py:107
  78.6 418.7 %reduce-scatter.2.cloned.1.call-start = ((), (), s32[]{:S(2)}) async-start(), calls=%async_computation.8 | async-start | bytes 4325376 | tf_op jit(solution)/shard_map/reduce_scatter | solution.py:132
Sparse Core Ops, SparseCore 0:
  36.7 32.6 all-gather.6
  72.5 103.7 all-gather.4
  178.5 37.0 all-gather.8
  217.6 39.2 all-gather.10
  262.0 235.2 reduce-scatter.1
where the time goes:
time: 504 us
  waiting for transfers between devices  403 us (80%)
  blocking collectives  65.7 us (13%)
  matrix products  14.8 us (3%)
  between operations  13.9 us (3%)
  other arithmetic  5.83 us (1%)
    reduce_scatter x1, waiting for transfers between devices, on_device(): lax.psum_scatter(lax.dot_general(head_out, out_buffer, (((1,), (1,)), (()...  235 us
    all_gather x1, waiting for transfers between devices, on_device(): normed = lax.all_gather(local_rows, 'tensor', axis=0, tiled=True)  96.7 us
    all_gather x1, waiting for transfers between devices, on_device(): lax.all_gather(output_slice, 'section', axis=0, tiled=True)  35.8 us
    all_gather x1, waiting for transfers between devices, on_device(): keyval_rows = lax.all_gather(keyval_slice, 'section', axis=0, tiled=True)  34.9 us
    all_to_all x1, blocking collectives, on_device(): lax.all_to_all(query_weight, 'tensor', split_axis=1, concat_axis=0, tiled...  28.5 us
    all_to_all x1, blocking collectives, on_device(): lax.all_to_all(spread_heads, 'tensor', split_axis=1, concat_axis=0, tiled...  19.7 us
    all_to_all x1, blocking collectives, on_device(): lax.all_to_all(output_weight, 'tensor', split_axis=1, concat_axis=0, tile...  17.6 us
  transfers between devices with their start and end apart: 5, of which 4 were waited for; matrix products, arithmetic and copies ran while one was open for 3% of the time, Pallas kernels for 0%

commit v1 on v0

v1 whole, which is shorter than its diff:
```python
import math

import jax
import jax.numpy as jnp
from jax import lax
from jax.sharding import Mesh, PartitionSpec as P

XL = ("x", "l")
HC = ("h", "c")
XLH = ("x", "l", "h")

QUERY_HEADS_LOCAL = 32
KEYVAL_HEADS = 4
HEAD_DIMENSION = 128

learn_rate = 0.015
beta_one = 0.5
beta_two = 0.9
adam_step = 1000.0
adam_eps = 1e-08
decay_rate = 0.1
norm_eps = 1e-06
rope_base = 1000000.0
masked_score = -1e30


def adam_update(current, gradient, moment, second):
    moment_new = beta_one * moment + (1.0 - beta_one) * gradient
    second_new = beta_two * second + (1.0 - beta_two) * gradient * gradient
    corrected = moment_new / (1.0 - beta_one**adam_step)
    denominator = jnp.sqrt(second_new / (1.0 - beta_two**adam_step)) + adam_eps
    return (current - learn_rate * (corrected / denominator + decay_rate * current)).astype(
        jnp.bfloat16
    )


def normalize(hidden, norm_gain):
    values = hidden.astype(jnp.float32)
    factor = lax.rsqrt(jnp.mean(values * values, axis=-1, keepdims=True) + norm_eps)
    return (values * factor * norm_gain).astype(jnp.bfloat16)


def swap_blocks(blocks, axes):
    return lax.all_to_all(blocks, axes, split_axis=0, concat_axis=0, tiled=True)


def partner(values):
    return lax.ppermute(values, "c", [(0, 1), (1, 0)])


def on_device(
    hidden,
    norm_gain,
    lengths,
    query_param,
    query_grad,
    query_moment,
    query_second,
    keyval_param,
    keyval_gradient,
    keyval_first_moment,
    keyval_second_moment,
    output_param,
    output_grad,
    output_moment,
    output_second,
):
    bf16, f32 = jnp.bfloat16, jnp.float32
    xl = lax.axis_size(XL)
    hc = lax.axis_size(HC)
    n_h, n_c, n_z = lax.axis_size("h"), lax.axis_size("c"), lax.axis_size("z")
    tokens, width = hidden.shape[1], hidden.shape[2]
    rows = query_param.shape[0]
    heads = QUERY_HEADS_LOCAL // hc
    head_cols = heads * HEAD_DIMENSION
    depth = width // xl

    query_weight = adam_update(query_param, query_grad, query_moment, query_second)
    keyval_weight = adam_update(
        keyval_param, keyval_gradient, keyval_first_moment, keyval_second_moment
    )
    query_blocks = query_weight.reshape(rows, hc, head_cols).transpose(1, 0, 2)
    keyval_blocks = (
        keyval_weight.reshape(rows, 2, KEYVAL_HEADS, HEAD_DIMENSION)
        .transpose(2, 0, 1, 3)
        .reshape(KEYVAL_HEADS, rows, 2 * HEAD_DIMENSION)
    )
    keyval_blocks = jnp.repeat(keyval_blocks, hc // KEYVAL_HEADS, axis=0)
    proj_blocks = swap_blocks(jnp.concatenate([query_blocks, keyval_blocks], axis=2), HC)
    proj_cols = proj_blocks.shape[2]
    proj_all = lax.all_gather(proj_blocks, "z", axis=0)
    proj_weight = (
        proj_all.reshape(n_z, n_h, n_c, rows, proj_cols)
        .transpose(2, 1, 0, 3, 4)
        .reshape(depth, proj_cols)
    )
    output_weight = adam_update(output_param, output_grad, output_moment, output_second)
    output_blocks = swap_blocks(
        output_weight.reshape(rows, hc, head_cols).transpose(1, 0, 2), HC
    )
    output_all = lax.all_gather(output_blocks, "z", axis=0)
    output_matrix = (
        output_all.reshape(n_z, n_h, n_c, rows, head_cols)
        .transpose(2, 1, 0, 3, 4)
        .reshape(depth, head_cols)
    )

    local_rows = normalize(hidden[0], norm_gain)
    row_blocks = local_rows.reshape(tokens, xl, 1, depth).transpose(1, 2, 0, 3)
    row_blocks = jnp.broadcast_to(row_blocks, (xl, n_h, tokens, depth))
    row_blocks = swap_blocks(row_blocks.reshape(xl * n_h, tokens, depth), XLH)
    here = row_blocks.reshape(xl, 1, n_h * tokens, depth)
    both = jnp.concatenate([here, partner(here)], axis=1)
    spread = n_c * n_h * tokens

    partial = jnp.dot(
        both.reshape(xl * spread, depth), proj_weight, preferred_element_type=f32
    ).astype(bf16)
    partial = swap_blocks(partial.reshape(xl, spread, proj_cols), XL)
    projected = jnp.sum(partial.astype(f32), axis=0).reshape(n_c, n_h * tokens, proj_cols)

    half = HEAD_DIMENSION // 2
    frequency = rope_base ** (-jnp.arange(half, dtype=f32) * 2.0 / HEAD_DIMENSION)
    local = jnp.arange(n_h * tokens)
    stride = n_z * tokens
    positions = (local // tokens) * stride + lax.axis_index("z") * tokens + local % tokens
    angles = positions.astype(f32)[:, None] * frequency[None, :]
    cosine = jnp.concatenate([jnp.cos(angles), jnp.cos(angles)], axis=-1)
    sine = jnp.concatenate([-jnp.sin(angles), jnp.sin(angles)], axis=-1)

    def rotary(values):
        swapped = jnp.concatenate([values[..., half:], values[..., :half]], axis=-1)
        return (values * cosine + swapped * sine).astype(bf16)

    key_rows = rotary(projected[:, :, head_cols : head_cols + HEAD_DIMENSION])
    value_rows = projected[:, :, head_cols + HEAD_DIMENSION :].astype(bf16)
    keyval_rows = jnp.concatenate([key_rows, value_rows], axis=-1)
    keyval_rows = swap_blocks(
        jnp.broadcast_to(keyval_rows[None], (n_z,) + keyval_rows.shape), "z"
    )
    keyval_rows = keyval_rows.transpose(1, 0, 2, 3).reshape(
        n_c, n_z * n_h * tokens, 2 * HEAD_DIMENSION
    )
    query_rows = jnp.concatenate(
        [
            rotary(projected[:, :, i * HEAD_DIMENSION : (i + 1) * HEAD_DIMENSION])
            for i in range(heads)
        ],
        axis=1,
    )

    scores = jnp.einsum(
        "cqd,ckd->cqk",
        query_rows,
        keyval_rows[:, :, :HEAD_DIMENSION],
        preferred_element_type=f32,
    ) / math.sqrt(HEAD_DIMENSION)
    key_at = jnp.arange(n_z * n_h * tokens)
    key_at = (
        (key_at // tokens % n_h) * stride + key_at // (n_h * tokens) * tokens + key_at % tokens
    )
    query_at = jnp.tile(positions, heads)
    valid = jnp.stack([lengths[0], partner(lengths)[0]])
    allowed = (key_at[None, :] <= query_at[:, None])[None] & (
        key_at[None, None, :] < valid[:, None, None]
    )
    scores = jnp.where(allowed, scores, masked_score)
    exponent = jnp.exp(scores - jnp.max(scores, axis=-1, keepdims=True))
    attention = (exponent / jnp.sum(exponent, axis=-1, keepdims=True)).astype(bf16)
    head_out = jnp.einsum(
        "cqk,ckd->cqd",
        attention,
        keyval_rows[:, :, HEAD_DIMENSION:],
        preferred_element_type=f32,
    ).astype(bf16)
    head_out = (
        head_out.reshape(n_c, heads, n_h * tokens, HEAD_DIMENSION)
        .transpose(0, 2, 1, 3)
        .reshape(spread, head_cols)
    )

    head_all = swap_blocks(jnp.broadcast_to(head_out[None], (xl,) + head_out.shape), XL)
    mixed = lax.dot_general(
        head_all.reshape(xl * spread, head_cols),
        output_matrix,
        (((1,), (1,)), ((), ())),
        preferred_element_type=f32,
    ).reshape(xl, n_c, n_h * tokens, depth)
    mixed = (mixed[:, 0] + partner(mixed[:, 1].astype(bf16)).astype(f32)).astype(bf16)
    mixed = swap_blocks(mixed.reshape(xl * n_h, tokens, depth), XLH)
    mixed = jnp.sum(mixed.reshape(xl, n_h, tokens, depth).astype(f32), axis=1).astype(bf16)
    return mixed.transpose(1, 0, 2).reshape(1, tokens, width)


def solution(mesh):
    fine = Mesh(mesh.devices.reshape(4, 2, 2, 4, 8), ("x", "l", "c", "h", "z"))
    section, tensor = ("x", "l", "c"), ("h", "z")
    by_row = P(section + tensor, None)
    return jax.shard_map(
        on_device,
        mesh=fine,
        in_specs=(P(section, tensor, None), P(), P(section)) + (by_row,) * 12,
        out_specs=P(section, tensor, None),
        check_vma=False,
    )
```

time: 504 us -> 190 us (0.38)
  waiting for transfers between devices: 403 us -> 67.4 us
  starting transfers between devices: 0.2 us -> 28 us
  matrix products: 14.8 us -> 3.71 us
  local copies, waits for them, and re-layouts: 0.52 us -> 5.88 us
    reduce_scatter x1 -> x0, waiting for transfers between devices: 235 us -> none  [on_device(): lax.psum_scatter(lax.dot_general(head_out, out_buffer, (((1,), (1,)), (()...]
    all_gather x4 -> x2, waiting for transfers between devices: 167 us -> 39.7 us  [the longest x1 22.3 us: on_device(): output_all = lax.all_gather(output_blocks, 'z', axis=0)]
    all_to_all x0 -> x4, waiting for transfers between devices: none -> 25.2 us  [swap_blocks(): return lax.all_to_all(blocks, axes, split_axis=0, concat_axis=0, tiled=True)]
    all_to_all x0 -> x4, starting transfers between devices: none -> 21.7 us  [swap_blocks(): return lax.all_to_all(blocks, axes, split_axis=0, concat_axis=0, tiled=True)]
    dot_general x4, matrix products: 14.8 us -> 3.35 us  [the longest x1 1.87 us: on_device(): jnp.dot(both.reshape(xl * spread, depth), proj_weight, preferred_element_...]
    ppermute x0 -> x3, starting transfers between devices: none -> 6.24 us  [partner(): return lax.ppermute(values, 'c', [(0, 1), (1, 0)])]
  transfers between devices with their start and end apart: 5 -> 9, of which waited for: 4 -> 6; matrix products, arithmetic and copies ran while one was open for 3% -> 6% of each run, Pallas kernels for 0% -> 0%
where the time goes in v1:
time: 190 us; the launch traced here: 188 us
  waiting for transfers between devices  67.4 us (35%)
  blocking collectives  63 us (33%)
  starting transfers between devices  28 us (15%)
  between operations  14.4 us (8%)
  local copies, waits for them, and re-layouts  5.88 us (3%)
  other arithmetic  5.25 us (3%)
  matrix products  3.71 us (2%)
    all_to_all x3, blocking collectives, swap_blocks(): return lax.all_to_all(blocks, axes, split_axis=0, concat_axis=0, tiled=True)  63 us
    all_to_all x4, waiting for transfers between devices, swap_blocks(): return lax.all_to_all(blocks, axes, split_axis=0, concat_axis=0, tiled=True)  25.2 us
    all_gather x1, waiting for transfers between devices, on_device(): output_all = lax.all_gather(output_blocks, 'z', axis=0)  22.3 us
    all_to_all x4, starting transfers between devices, swap_blocks(): return lax.all_to_all(blocks, axes, split_axis=0, concat_axis=0, tiled=True)  21.7 us
    all_gather x1, waiting for transfers between devices, on_device(): proj_all = lax.all_gather(proj_blocks, 'z', axis=0)  17.3 us
    ppermute x3, starting transfers between devices, partner(): return lax.ppermute(values, 'c', [(0, 1), (1, 0)])  6.24 us
  transfers between devices with their start and end apart: 9, of which 6 were waited for; matrix products, arithmetic and copies ran while one was open for 6% of the time, Pallas kernels for 0%

profile of v1, /device:TPU:6, one launch (start us, length us, event | category | flops | bytes accessed | tf_op | source)
XLA Modules:
  0.0 187.6 jit_solution(2350919999768007838)
XLA Ops:
  6.5 1.0 fusion.41
  7.8 1.4 fusion.22
  9.3 17.7 %all_to_all.35 = bf16[8,16,768]{2,1,0:T(8,128)(2,1)} all-to-all(bf16[8,16,768]{2,1,0:T(8,128)(2,1)S(1)} %copy.44), channel_id=1, replica_groups=mesh['x'=4,'l'=2,'c'=2,'h'=4,'z'=8] {'h','c'}, dimensions={0} | all-to-all | bytes 393216 | tf_op jit(solution)/shard_map/all_to_all | solution.py:44
  27.0 0.2 multiply_reduce_fusion
  27.2 0.1 fusion.23
  27.3 0.1 broadcast_in_dim.16
  27.4 20.2 %all_to_all.36 = bf16[32,8,1024]{2,1,0:T(8,128)(2,1)S(1)} all-to-all(bf16[32,8,1024]{2,1,0:T(8,128)(2,1)S(1)} %bitcast.72), channel_id=1, replica_groups=mesh['x'=4,'l'=2,'c'=2,'h'=4,'z'=8] {'x','l','h'}, dimensions={0} | all-to-all | bytes 1048576 | tf_op jit(solution)/shard_map/all_to_all | solution.py:44
  47.5 1.9 %collective-permute-start.1 = (bf16[8,1,32,1024]{3,2,1,0:T(8,128)(2,1)S(1)}, bf16[8,1,32,1024]{3,2,1,0:T(8,128)(2,1)S(1)}, u32[]{:S(2)}, u32[]{:S(2)}) collective-permute-start(bf16[8,1,32,1024]{3,2,1,0:T(8,128)(2,1)S(1)} %bitcast.73), channel_id=1, source_target_pairs={{0,32},{32,0},{1,33},{33,1},{2,34},{34,2},{3,35},{35,3},{4,36},{36... | collective-permute-start | bytes 1572872 | tf_op jit(solution)/shard_map/ppermute | solution.py:48
  49.4 2.4 %collective-permute-start = (s32[1]{0:T(128)}, s32[1]{0:T(128)}, u32[]{:S(2)}, u32[]{:S(2)}) collective-permute-start(s32[1]{0:T(128)} %param.17), channel_id=1, source_target_pairs={{0,32},{32,0},{1,33},{33,1},{2,34},{34,2},{3,35},{35,3},{4,36},{36... | collective-permute-start | bytes 20 | tf_op jit(solution)/shard_map/ppermute | solution.py:48
  52.5 0.1 le.20
  52.6 0.1 pad_maximum_fusion
  52.7 17.3 %all-gather.5.cloned.1.call-done = bf16[64,16,768]{2,1,0:T(8,128)(2,1)} async-done(((bf16[8,16,768]{2,1,0:T(8,128)(2,1)}), bf16[64,16,768]{2,1,0:T(8,128)(2,1)}) %all-gather.5.cloned.1.call-update) | async-done | bytes 1572880 | tf_op jit(solution)/shard_map/all_gather | solution.py:91
  70.1 1.5 copy.45
  71.6 1.9 convolution_convert_fusion
  73.5 5.9 %all-to-all-start.2 = ((bf16[8,64,768]{2,1,0:T(8,128)(2,1)}), bf16[8,64,768]{2,1,0:T(8,128)(2,1)S(1)}, u32[]{:S(2)}, u32[]{:S(2)}) async-start(bf16[8,64,768]{2,1,0:T(8,128)(2,1)} %bitcast.11), calls=%async_computation.2 | async-start | bytes 1572864 | tf_op jit(solution)/shard_map/all_to_all | solution.py:44
  79.4 0.2 fusion.21
  79.6 0.7 copy.48
  80.3 0.1 multiply_cosine_fusion
  80.5 0.1 pad_maximum_fusion.3
  80.5 0.1 pad_maximum_fusion.4
  80.6 6.6 %all-to-all-done.2 = bf16[8,64,768]{2,1,0:T(8,128)(2,1)S(1)} async-done(((bf16[8,64,768]{2,1,0:T(8,128)(2,1)}), bf16[8,64,768]{2,1,0:T(8,128)(2,1)S(1)}, u32[]{:S(2)}, u32[]{:S(2)}) %all-to-all-start.2) | async-done | bytes 786464 | tf_op jit(solution)/shard_map/all_to_all | solution.py:44
  87.2 5.9 %all-to-all-start.5 = ((bf16[8,16,512]{2,1,0:T(8,128)(2,1)}), bf16[8,16,512]{2,1,0:T(8,128)(2,1)S(1)}, u32[]{:S(2)}, u32[]{:S(2)}) async-start(bf16[8,16,512]{2,1,0:T(8,128)(2,1)} %copy.48), calls=%async_computation.5 | async-start | bytes 262144 | tf_op jit(solution)/shard_map/all_to_all | solution.py:44
  93.1 0.1 convert_reduce_fusion
  93.2 0.1 fusion.75
  93.3 0.1 fusion.51
  93.5 9.2 %all-to-all-done.5 = bf16[8,16,512]{2,1,0:T(8,128)(2,1)S(1)} async-done(((bf16[8,16,512]{2,1,0:T(8,128)(2,1)}), bf16[8,16,512]{2,1,0:T(8,128)(2,1)S(1)}, u32[]{:S(2)}, u32[]{:S(2)}) %all-to-all-start.5) | async-done | bytes 131104 | tf_op jit(solution)/shard_map/all_to_all | solution.py:44
  102.7 0.7 broadcast_in_dim.18
  103.4 4.1 %all-to-all-start.3 = ((bf16[8,2,32,256]{3,2,1,0:T(8,128)(2,1)}), bf16[8,2,32,256]{3,2,1,0:T(8,128)(2,1)S(1)}, u32[]{:S(2)}, u32[]{:S(2)}) async-start(bf16[8,2,32,256]{3,2,1,0:T(8,128)(2,1)} %broadcast_in_dim.18), calls=%async_computation.3 | async-start | bytes 524288 | tf_op jit(solution)/shard_map/all_to_all | solution.py:44
  107.5 0.0 all-gather.7.cloned.1.call-start
  107.6 0.1 broadcast_compare_fusion
  107.7 0.6 all-gather.7.cloned.1.call-update
  108.3 0.7 pad_add_fusion
  109.0 0.1 broadcast_compare_fusion.1
  109.1 9.5 %all-to-all-done.3 = bf16[8,2,32,256]{3,2,1,0:T(8,128)(2,1)S(1)} async-done(((bf16[8,2,32,256]{3,2,1,0:T(8,128)(2,1)}), bf16[8,2,32,256]{3,2,1,0:T(8,128)(2,1)S(1)}, u32[]{:S(2)}, u32[]{:S(2)}) %all-to-all-start.3) | async-done | bytes 262176 | tf_op jit(solution)/shard_map/all_to_all | solution.py:44
  118.6 0.4 fusion.76
  118.9 0.2 fusion.2
  119.1 0.6 convolution_convert_fusion.1
  119.8 0.9 broadcast_in_dim.21
  120.6 5.8 %all-to-all-start.4 = ((bf16[8,64,512]{2,1,0:T(8,128)(2,1)}), bf16[8,64,512]{2,1,0:T(8,128)(2,1)S(1)}, u32[]{:S(2)}, u32[]{:S(2)}) async-start(bf16[8,64,512]{2,1,0:T(8,128)(2,1)} %broadcast_in_dim.21), calls=%async_computation.4 | async-start | bytes 1048576 | tf_op jit(solution)/shard_map/all_to_all | solution.py:44
  126.4 22.3 %all-gather.7.cloned.1.call-done = bf16[64,16,512]{2,1,0:T(8,128)(2,1)} async-done(((bf16[8,16,512]{2,1,0:T(8,128)(2,1)}), bf16[64,16,512]{2,1,0:T(8,128)(2,1)}) %all-gather.7.cloned.1.call-update) | async-done | bytes 1048592 | tf_op jit(solution)/shard_map/all_gather | solution.py:101
  148.8 1.3 copy.49
  150.1 0.7 fusion.81
  150.8 0.1 fusion.6
  150.9 1.9 %collective-permute-start.2 = (bf16[8,32,1024]{2,1,0:T(8,128)(2,1)S(1)}, bf16[8,32,1024]{2,1,0:T(8,128)(2,1)S(1)}, u32[]{:S(2)}, u32[]{:S(2)}) collective-permute-start(bf16[8,32,1024]{2,1,0:T(8,128)(2,1)S(1)} %fusion.6), channel_id=1, source_target_pairs={{0,32},{32,0},{1,33},{33,1},{2,34},{34,2},{3,35},{35,3},{4,36},{36... | collective-permute-start | bytes 1572872 | tf_op jit(solution)/shard_map/ppermute | solution.py:48
  152.8 1.9 collective-permute-done.2
  154.7 0.1 fusion.5
  154.9 25.2 %all_to_all.37 = bf16[32,8,1024]{2,1,0:T(8,128)(2,1)S(1)} all-to-all(bf16[32,8,1024]{2,1,0:T(8,128)(2,1)S(1)} %bitcast.75), channel_id=1, replica_groups=mesh['x'=4,'l'=2,'c'=2,'h'=4,'z'=8] {'x','l','h'}, dimensions={0} | all-to-all | bytes 1048576 | tf_op jit(solution)/shard_map/all_to_all | solution.py:44
  180.0 0.7 bitcast_reduce_fusion
  (40 shorter events, 0.5 us)
Async XLA Ops:
  6.5 63.5 %all-gather.5.cloned.1.call-start = ((), (), s32[]{:S(2)}) async-start(), calls=%async_computation.7 | async-start | bytes 1769472 | tf_op jit(solution)/shard_map/all_gather | solution.py:91
  7.6 19.4 %copy-start.6 = (f32[8192]{0:T(1024)S(1)}, f32[8192]{0:T(1024)}, u32[]{:S(2)}) copy-start(f32[8192]{0:T(1024)} %param.16) | copy-start | bytes 98308
  7.7 19.3 %copy-start = (bf16[1,8,8192]{2,1,0:T(8,128)(2,1)S(1)}, bf16[1,8,8192]{2,1,0:T(8,128)(2,1)}, u32[]{:S(2)}) copy-start(bf16[1,8,8192]{2,1,0:T(8,128)(2,1)} %param.15) | copy-start | bytes 393220
  47.5 5.1 %collective-permute-start.1 = (bf16[8,1,32,1024]{3,2,1,0:T(8,128)(2,1)S(1)}, bf16[8,1,32,1024]{3,2,1,0:T(8,128)(2,1)S(1)}, u32[]{:S(2)}, u32[]{:S(2)}) collective-permute-start(bf16[8,1,32,1024]{3,2,1,0:T(8,128)(2,1)S(1)} %bitcast.73), channel_id=1, source_target_pairs={{0,32},{32,0},{1,33},{33,1},{2,34},{34,2},{3,35},{35,3},{4,36},{36... | collective-permute-start | bytes 1572872 | tf_op jit(solution)/shard_map/ppermute | solution.py:48
  49.4 58.8 %collective-permute-start = (s32[1]{0:T(128)}, s32[1]{0:T(128)}, u32[]{:S(2)}, u32[]{:S(2)}) collective-permute-start(s32[1]{0:T(128)} %param.17), channel_id=1, source_target_pairs={{0,32},{32,0},{1,33},{33,1},{2,34},{34,2},{3,35},{35,3},{4,36},{36... | collective-permute-start | bytes 20 | tf_op jit(solution)/shard_map/ppermute | solution.py:48
  73.5 5.9 %copy-start.2 = (f32[16,4096]{1,0:T(8,128)S(1)}, f32[16,4096]{1,0:T(8,128)}, u32[]{:S(2)}) copy-start(f32[16,4096]{1,0:T(8,128)} %param.26) | copy-start | bytes 786436
  73.5 5.9 %copy-start.3 = (f32[16,4096]{1,0:T(8,128)S(1)}, f32[16,4096]{1,0:T(8,128)}, u32[]{:S(2)}) copy-start(f32[16,4096]{1,0:T(8,128)} %param.27) | copy-start | bytes 786436
  73.5 5.9 %copy-start.4 = (f32[16,4096]{1,0:T(8,128)S(1)}, f32[16,4096]{1,0:T(8,128)}, u32[]{:S(2)}) copy-start(f32[16,4096]{1,0:T(8,128)} %param.29) | copy-start | bytes 786436
  73.5 5.9 %copy-start.5 = (f32[16,4096]{1,0:T(8,128)S(1)}, f32[16,4096]{1,0:T(8,128)}, u32[]{:S(2)}) copy-start(f32[16,4096]{1,0:T(8,128)} %param.28) | copy-start | bytes 786436
  73.5 13.7 %all-to-all-start.2 = ((bf16[8,64,768]{2,1,0:T(8,128)(2,1)}), bf16[8,64,768]{2,1,0:T(8,128)(2,1)S(1)}, u32[]{:S(2)}, u32[]{:S(2)}) async-start(bf16[8,64,768]{2,1,0:T(8,128)(2,1)} %bitcast.11), calls=%async_computation.2 | async-start | bytes 1572864 | tf_op jit(solution)/shard_map/all_to_all | solution.py:44
  87.2 15.5 %all-to-all-start.5 = ((bf16[8,16,512]{2,1,0:T(8,128)(2,1)}), bf16[8,16,512]{2,1,0:T(8,128)(2,1)S(1)}, u32[]{:S(2)}, u32[]{:S(2)}) async-start(bf16[8,16,512]{2,1,0:T(8,128)(2,1)} %copy.48), calls=%async_computation.5 | async-start | bytes 262144 | tf_op jit(solution)/shard_map/all_to_all | solution.py:44
  102.7 5.0 %copy-start.1 = (bf16[8,16,512]{2,1,0:T(8,128)(2,1)}, bf16[8,16,512]{2,1,0:T(8,128)(2,1)S(1)}, u32[]{:S(2)}) copy-start(bf16[8,16,512]{2,1,0:T(8,128)(2,1)S(1)} %all-to-all-done.5) | copy-start | bytes 393220
  103.4 15.1 %all-to-all-start.3 = ((bf16[8,2,32,256]{3,2,1,0:T(8,128)(2,1)}), bf16[8,2,32,256]{3,2,1,0:T(8,128)(2,1)S(1)}, u32[]{:S(2)}, u32[]{:S(2)}) async-start(bf16[8,2,32,256]{3,2,1,0:T(8,128)(2,1)} %broadcast_in_dim.18), calls=%async_computation.3 | async-start | bytes 524288 | tf_op jit(solution)/shard_map/all_to_all | solution.py:44
  107.5 41.2 %all-gather.7.cloned.1.call-start = ((), (), s32[]{:S(2)}) async-start(), calls=%async_computation.8 | async-start | bytes 1179648 | tf_op jit(solution)/shard_map/all_gather | solution.py:101
  120.6 29.5 %all-to-all-start.4 = ((bf16[8,64,512]{2,1,0:T(8,128)(2,1)}), bf16[8,64,512]{2,1,0:T(8,128)(2,1)S(1)}, u32[]{:S(2)}, u32[]{:S(2)}) async-start(bf16[8,64,512]{2,1,0:T(8,128)(2,1)} %broadcast_in_dim.21), calls=%async_computation.4 | async-start | bytes 1048576 | tf_op jit(solution)/shard_map/all_to_all | solution.py:44
  150.9 3.8 %collective-permute-start.2 = (bf16[8,32,1024]{2,1,0:T(8,128)(2,1)S(1)}, bf16[8,32,1024]{2,1,0:T(8,128)(2,1)S(1)}, u32[]{:S(2)}, u32[]{:S(2)}) collective-permute-start(bf16[8,32,1024]{2,1,0:T(8,128)(2,1)S(1)} %fusion.6), channel_id=1, source_target_pairs={{0,32},{32,0},{1,33},{33,1},{2,34},{34,2},{3,35},{35,3},{4,36},{36... | collective-permute-start | bytes 1572872 | tf_op jit(solution)/shard_map/ppermute | solution.py:48
Sparse Core Ops, SparseCore 0:
  27.1 42.9 all-gather.4
  110.4 38.3 all-gather.6
